TPU v7x, 256 devices: a whole 4x4x8 slice. The times are simulated.
256 devices in a mesh: heads: 16 (over x_lo, y, core), keys: 16 (over z, x_hi).
Axes of the slice: x: 4 (x_hi: 2, x_lo: 2; x = x_hi * 2 + x_lo), y: 4, z: 8, core: 2. Of those that a mesh axis runs over, the one named last changes fastest.
Arguments:
- main_query: bfloat16 [256, 128, 576], P(None, 'heads'), may hold values from -5 to 5
- latent_keys: bfloat16 [32768, 576], P('keys'), may hold values from -16 to 16
- index_query: bfloat16 [256, 64, 128], P('heads'), may hold values from -1 to 1
- index_keys: bfloat16 [32768, 128], P('keys'), may hold values from -20 to 20
- index_weight: float32 [256, 64], P('heads'), may hold values from -0.15 to 1
- query_pos: int32 [256], replicated, may hold values from 4096 to 32767, as said below
- kl_weight: float32 [256], P('heads'), may hold values from 2 to 16
Outputs:
- index_query_grad: float32 [256, 64, 128], P('heads')
- index_key_grad: float32 [32768, 128], P('keys')
- index_weight_grad: float32 [256, 64], P('heads')
Inputs may be any that keep to these rules, and one draw needn't show every extreme that they name: Query q sees the keys at positions 0 to query_pos[q]; some query sees all 32768 keys and some sees exactly the first 4097.
All inputs are finite; a program needn't handle non-finite values.
Results may differ from a plain program's by a relative error of at most 0.005.
Values sent between devices are 32-bit elements; how exact they have to be, the bound alone decides.
A program may use at most 128 MiB of HBM per device.

v0:
```python
import jax
import jax.numpy as jnp
from jax import lax
from jax.sharding import PartitionSpec as P

H = 128
softmax_scale = 192.0 ** (-0.5)
masked_fill = -1e30


def contract_last(left_side, right_side):
    return lax.dot_general(
        left_side, right_side, (((1,), (1,)), ((), ())), preferred_element_type=jnp.float32
    )


def shards(main_query, latent_keys, index_query, index_keys, index_weight, query_pos, kl_weight):
    query_count, head_local, feature_width = main_query.shape
    key_local = latent_keys.shape[0]
    row_local, index_heads, index_width = index_query.shape
    key_first = lax.axis_index("keys") * key_local
    key_index = key_first + lax.iota(jnp.int32, key_local)
    visible = key_index[None, :] <= query_pos[:, None]
    row_first = lax.axis_index("heads") * row_local
    row_pos = lax.dynamic_slice_in_dim(query_pos, row_first, row_local)
    row_visible = key_index[None, :] <= row_pos[:, None]
    main_scores = contract_last(
        main_query.reshape(query_count * head_local, feature_width), latent_keys
    )
    main_scores = main_scores.reshape(query_count, head_local, key_local) * softmax_scale
    main_scores = jnp.where(visible[:, None, :], main_scores, masked_fill)
    index_logits = contract_last(
        index_query.reshape(row_local * index_heads, index_width), index_keys
    )
    index_logits = index_logits.reshape(row_local, index_heads, key_local)
    active = jnp.maximum(index_logits, 0.0)
    index_scores = jnp.einsum("qj,qjk->qk", index_weight, active, precision=lax.Precision.HIGHEST)
    index_scores = jnp.where(row_visible, index_scores, masked_fill)
    main_local = jnp.max(main_scores, axis=2)
    index_local = jnp.max(index_scores, axis=1)
    main_maxima, index_maxima = lax.pmax((main_local, index_local), "keys")
    main_sum = jnp.sum(
        jnp.where(visible[:, None, :], jnp.exp(main_scores - main_maxima[:, :, None]), 0.0), axis=2
    )
    index_sum = jnp.sum(
        jnp.where(row_visible, jnp.exp(index_scores - index_maxima[:, None]), 0.0), axis=1
    )
    main_totals, index_totals = lax.psum((main_sum, index_sum), "keys")
    main_probs = (
        jnp.where(visible[:, None, :], jnp.exp(main_scores - main_maxima[:, :, None]), 0.0)
        / main_totals[:, :, None]
    )
    partial_value = jnp.sum(main_probs, axis=1)
    summed = lax.psum(partial_value, "heads")
    target = lax.dynamic_slice_in_dim(summed, row_first, row_local, 0)
    target = target / H
    index_probs = (
        jnp.where(row_visible, jnp.exp(index_scores - index_maxima[:, None]), 0.0)
        / index_totals[:, None]
    )
    index_delta = kl_weight[:, None] * (index_probs - target)
    weight_grad = jnp.einsum("qk,qjk->qj", index_delta, active, precision=lax.Precision.HIGHEST)
    slopes = jnp.where(
        index_logits > 0.0, index_delta[:, None, :] * index_weight[:, :, None], 0.0
    ).astype(jnp.bfloat16)
    flattened = slopes.reshape(row_local * index_heads, key_local)
    query_grad = jnp.dot(flattened, index_keys, preferred_element_type=jnp.float32).reshape(
        row_local, index_heads, index_width
    )
    key_grad = lax.dot_general(
        flattened,
        index_query.reshape(row_local * index_heads, index_width),
        (((0,), (0,)), ((), ())),
        preferred_element_type=jnp.float32,
    )
    query_grad, weight_grad = lax.psum((query_grad, weight_grad), "keys")
    key_grad = lax.psum(key_grad, "heads")
    return (query_grad, key_grad, weight_grad)


def solution(mesh):
    placed = (
        P(None, "heads", None),
        P("keys", None),
        P("heads", None, None),
        P("keys", None),
        P("heads", None),
        P(),
        P("heads"),
    )
    return jax.shard_map(
        shards,
        mesh=mesh,
        in_specs=placed,
        out_specs=(P("heads", None, None), P("keys", None), P("heads", None)),
        check_vma=False,
    )
```

profile of v0, /device:TPU:1, one launch (start us, length us, event | category | flops | bytes accessed | tf_op | source)
XLA Modules:
  0.0 565.1 jit_solution(11761084762094805328)
XLA Ops:
  7.2 0.0 copy-start
  7.2 0.0 copy-start.4
  7.2 0.0 all-reduce.6.cloned.1.call-start
  7.3 0.9 dynamic_slice.6
  8.2 0.0 copy-start.6
  8.2 1.0 broadcast_compare_fusion
  9.2 0.0 copy-start.8
  9.2 3.3 fusion.8
  12.5 0.0 copy-start.1
  12.6 3.2 copy-done.1
  15.8 0.0 copy-done.4
  15.8 4.6 fusion.4
  20.4 0.2 fusion.28
  20.6 0.0 copy-done
  20.6 0.0 copy-done.8
  20.6 11.6 %fusion = (f32[256,8]{0,1:T(8,128)S(1)}, f32[256,8,2048]{2,0,1:T(8,128)}) fusion(pred[256,2048]{1,0:T(8,128)(4,1)S(1)} %broadcast_compare_fusion, bf16[256,8,576]{0,2,1:T(8,128)(2,1)S(1)} %copy-done, bf16[2048,576]{0,1:T(8,128)(2,1)S(1)} %copy-done.8), kind=kOutput, calls=%fused_computation.3 | convolution fusion | flops 4844419072 | bytes 22028288 | tf_op jit(solution)/shard_map/dot_general | solution.py:12
  32.2 39.7 %all-reduce.1 = (f32[256,8]{0,1:T(8,128)S(1)}, f32[16]{0:T(128)S(1)}) all-reduce(f32[256,8]{0,1:T(8,128)S(1)} %get-tuple-element.7, f32[16]{0:T(128)S(1)} %fusion.28), channel_id=1, replica_groups=mesh['heads'=16,'keys'=16] {'keys'}, use_global_device_ids=true, to_apply=%region_5.6 | all-reduce | flops 2064 | bytes 16512 | tf_op jit(solution)/shard_map/pmax | solution.py:41
  71.9 0.0 copy-start.7
  71.9 0.0 copy-done.6
  71.9 0.2 fusion.29
  72.1 8.4 %fusion.1 = f32[256,8]{0,1:T(8,128)S(1)} fusion(f32[256,8,2048]{2,0,1:T(8,128)} %get-tuple-element.8, f32[256,8]{0,1:T(8,128)S(1)} %get-tuple-element.5, pred[256,2048]{1,0:T(8,128)(4,1)S(1)} %broadcast_compare_fusion), kind=kLoop, calls=%fused_computation.4 | loop fusion | flops 20969472 | bytes 17317888 | tf_op jit(solution)/shard_map/reduce_sum | solution.py:42
  80.5 0.0 copy-done.7
  80.5 31.6 %all-reduce = (f32[256,8]{0,1:T(8,128)}, f32[16]{0:T(128)}) all-reduce(f32[256,8]{0,1:T(8,128)S(1)} %fusion.1, f32[16]{0:T(128)S(1)} %fusion.29), channel_id=1, replica_groups=mesh['heads'=16,'keys'=16] {'keys'}, use_global_device_ids=true, to_apply=%region_7.8 | all-reduce | flops 2064 | bytes 16512 | tf_op jit(solution)/shard_map/psum | solution.py:48
  112.2 0.0 copy-start.2
  112.2 10.2 %divide_reduce_fusion = f32[256,2048]{1,0:T(8,128)} fusion(f32[256,8,2048]{2,0,1:T(8,128)} %get-tuple-element.8, f32[256,8]{0,1:T(8,128)} %get-tuple-element.3, f32[256,8]{0,1:T(8,128)S(1)} %get-tuple-element.5, pred[256,2048]{1,0:T(8,128)(4,1)S(1)} %broadcast_compare_fusion), kind=kLoop, calls=%fused_computation.2 | loop fusion | flops 24641536 | bytes 19415040 | tf_op jit(solution)/shard_map/reduce_sum | solution.py:53
  122.4 0.0 all-reduce.6.cloned.1.call-update
  122.4 0.0 all-reduce.8.cloned.1.call-start
  122.4 140.4 %all-reduce.6.cloned.1.call-done = f32[256,2048]{1,0:T(8,128)} async-done(((f32[256,2048]{1,0:T(8,128)}), f32[256,2048]{1,0:T(8,128)}) %all-reduce.6.cloned.1.call-update) | async-done | bytes 2097168 | tf_op jit(solution)/shard_map/psum | solution.py:54
  262.9 1.1 subtract_multiply_fusion
  263.9 0.0 copy-done.2
  264.0 0.0 copy-start.3
  264.0 0.0 copy-start.5
  264.0 3.1 fusion.7
  267.1 0.0 all-reduce.8.cloned.1.call-update
  267.1 0.0 all-reduce.10.cloned.1.call-start
  267.2 0.0 copy-done.3
  267.2 0.0 copy-done.5
  267.2 3.6 fusion.19
  270.8 0.0 all-reduce.10.cloned.1.call-update
  270.8 9.0 %fusion.2 = f32[16,1,64]{2,1,0:T(1,128)S(1)} fusion(f32[16,64,2048]{2,1,0:T(8,128)} %copy-done.1, f32[16,2048,1]{1,0,2:T(8,128)S(1)} %bitcast.34), kind=kOutput, calls=%fused_computation.8 | convolution fusion | flops 27262976 | bytes 8523776 | tf_op jit(solution)/shard_map/qk,qjk->qj/dot_general | solution.py:62
  279.8 36.5 %psum.47 = f32[16,64]{1,0:T(8,128)} all-reduce(f32[16,64]{1,0:T(8,128)S(1)} %bitcast.35), channel_id=1, replica_groups=mesh['heads'=16,'keys'=16] {'keys'}, use_global_device_ids=true, to_apply=%region_12.13 | all-reduce | flops 1024 | bytes 8192 | tf_op jit(solution)/shard_map/psum | solution.py:76
  316.4 100.5 %all-reduce.8.cloned.1.call-done = f32[16,64,128]{2,1,0:T(8,128)} async-done(((f32[16,64,128]{2,1,0:T(8,128)}), f32[16,64,128]{2,1,0:T(8,128)}) %all-reduce.8.cloned.1.call-update) | async-done | bytes 524304 | tf_op jit(solution)/shard_map/psum | solution.py:76
  416.9 137.6 %all-reduce.10.cloned.1.call-done = f32[2048,128]{1,0:T(8,128)} async-done(((f32[2048,128]{1,0:T(8,128)}), f32[2048,128]{1,0:T(8,128)}) %all-reduce.10.cloned.1.call-update) | async-done | bytes 1048592 | tf_op jit(solution)/shard_map/psum | solution.py:77
  554.5 1.9 copy.28
  556.3 2.3 copy.29
  (1 shorter events, 0.0 us)
Async XLA Ops:
  7.2 13.4 %copy-start = (bf16[256,8,576]{0,2,1:T(8,128)(2,1)S(1)}, bf16[256,8,576]{0,2,1:T(8,128)(2,1)}, u32[]{:S(2)}) copy-start(bf16[256,8,576]{0,2,1:T(8,128)(2,1)} %param.7) | copy-start | bytes 7077892
  7.2 8.6 %copy-start.4 = (f32[16,64]{1,0:T(8,128)S(1)}, f32[16,64]{1,0:T(8,128)}, u32[]{:S(2)}) copy-start(f32[16,64]{1,0:T(8,128)} %param.11) | copy-start | bytes 12292
  7.2 255.7 %all-reduce.6.cloned.1.call-start = ((), (), s32[]{:S(2)}) async-start(), calls=%async_computation | async-start | bytes 4194304 | tf_op jit(solution)/shard_map/psum | solution.py:54
  8.2 63.8 %copy-start.6 = (s32[16]{0:T(128)}, s32[16]{0:T(128)S(1)}, u32[]{:S(2)}) copy-start(s32[16]{0:T(128)S(1)} %dynamic_slice.6) | copy-start | bytes 196
  9.2 11.4 %copy-start.8 = (bf16[2048,576]{0,1:T(8,128)(2,1)S(1)}, bf16[2048,576]{0,1:T(8,128)(2,1)}, u32[]{:S(2)}) copy-start(bf16[2048,576]{0,1:T(8,128)(2,1)} %param.8) | copy-start | bytes 7077892
  12.5 3.2 copy-start.1
  71.9 8.6 %copy-start.7 = (f32[16]{0:T(128)}, f32[16]{0:T(128)S(1)}, u32[]{:S(2)}) copy-start(f32[16]{0:T(128)S(1)} %get-tuple-element.6) | copy-start | bytes 196
  112.2 151.8 %copy-start.2 = (bf16[2048,128]{1,0:T(8,128)(2,1)S(1)}, bf16[2048,128]{1,0:T(8,128)(2,1)}, u32[]{:S(2)}) copy-start(bf16[2048,128]{1,0:T(8,128)(2,1)} %param.10) | copy-start | bytes 1572868
  122.4 294.5 %all-reduce.8.cloned.1.call-start = ((), (), s32[]{:S(2)}) async-start(), calls=%async_computation.1 | async-start | bytes 1048576 | tf_op jit(solution)/shard_map/psum | solution.py:76
  264.0 3.2 copy-start.3
  264.0 3.2 copy-start.5
  267.1 287.3 %all-reduce.10.cloned.1.call-start = ((), (), s32[]{:S(2)}) async-start(), calls=%async_computation.2 | async-start | bytes 2097152 | tf_op jit(solution)/shard_map/psum | solution.py:77
Sparse Core Ops, SparseCore 0:
  122.5 140.3 all-reduce.5
  267.3 149.5 all-reduce.7
  420.1 134.3 all-reduce.9
where the time goes:
time: 566 us; the launch traced here: 565 us
  waiting for transfers between devices  379 us (67%)
  blocking collectives  108 us (19%)
  matrix products  35.3 us (6%)
  other arithmetic  21.1 us (4%)
  between operations  13.9 us (2%)
  local copies, waits for them, and re-layouts  8.32 us (1%)
    psum x1, waiting for transfers between devices, shards(): summed = lax.psum(partial_value, 'heads')  140 us
    psum x1, waiting for transfers between devices, shards(): key_grad = lax.psum(key_grad, 'heads')  138 us
    psum x1, waiting for transfers between devices, shards(): query_grad, weight_grad = lax.psum((query_grad, weight_grad), 'keys')  101 us
    pmax x1, blocking collectives, shards(): main_maxima, index_maxima = lax.pmax((main_local, index_local), 'keys')  39.7 us
    psum x1, blocking collectives, shards(): query_grad, weight_grad = lax.psum((query_grad, weight_grad), 'keys')  36.5 us
    psum x1, blocking collectives, shards(): main_totals, index_totals = lax.psum((main_sum, index_sum), 'keys')  31.6 us
    dot_general x2, matrix products, contract_last(): lax.dot_general(left_side, right_side, (((1,), (1,)), ((), ())), preferre...  15 us
  transfers between devices with their start and end apart: 3, of which 3 were waited for; matrix products, arithmetic and copies ran while one was open for 2% of the time, Pallas kernels for 0%

commit v1 on v0

--- a/solution.py
+++ b/solution.py
@@ -6,6 +6,11 @@
 H = 128
 softmax_scale = 192.0 ** (-0.5)
 masked_fill = -1e30
+
+
+def gather_and_add(value, name):
+    parts = lax.all_gather(value, name)
+    return jnp.sum(parts, axis=0)
 
 
 def contract_last(left_side, right_side):
@@ -51,7 +56,7 @@
         / main_totals[:, :, None]
     )
     partial_value = jnp.sum(main_probs, axis=1)
-    summed = lax.psum(partial_value, "heads")
+    summed = gather_and_add(partial_value, "heads")
     target = lax.dynamic_slice_in_dim(summed, row_first, row_local, 0)
     target = target / H
     index_probs = (

time: 566 us -> 620 us (1.095)
  waiting for transfers between devices: 379 us -> 424 us
  other arithmetic: 21.1 us -> 32 us
    all_gather x0 -> x1, waiting for transfers between devices: none -> 186 us  [gather_and_add(): parts = lax.all_gather(value, name)]
    psum x1 -> x0, waiting for transfers between devices: 140 us -> none  [shards(): summed = lax.psum(partial_value, 'heads')]
    reduce_sum x0 -> x1, other arithmetic: none -> 11.9 us  [gather_and_add(): return jnp.sum(parts, axis=0)]
where the time goes in v1:
time: 620 us
  waiting for transfers between devices  424 us (68%)
  blocking collectives  108 us (17%)
  matrix products  33.2 us (5%)
  other arithmetic  32 us (5%)
  between operations  14 us (2%)
  local copies, waits for them, and re-layouts  8.59 us (1%)
    all_gather x1, waiting for transfers between devices, gather_and_add(): parts = lax.all_gather(value, name)  186 us
    psum x1, waiting for transfers between devices, shards(): key_grad = lax.psum(key_grad, 'heads')  138 us
    psum x1, waiting for transfers between devices, shards(): query_grad, weight_grad = lax.psum((query_grad, weight_grad), 'keys')  101 us
    pmax x1, blocking collectives, shards(): main_maxima, index_maxima = lax.pmax((main_local, index_local), 'keys')  39.7 us
    psum x1, blocking collectives, shards(): query_grad, weight_grad = lax.psum((query_grad, weight_grad), 'keys')  36.7 us
    psum x1, blocking collectives, shards(): main_totals, index_totals = lax.psum((main_sum, index_sum), 'keys')  31.5 us
    dot_general x2, matrix products, contract_last(): lax.dot_general(left_side, right_side, (((1,), (1,)), ((), ())), preferre...  14.9 us
  transfers between devices with their start and end apart: 3, of which 3 were waited for; matrix products, arithmetic and copies ran while one was open for 2% of the time, Pallas kernels for 0%

profile of v1, /device:TPU:1, one launch (start us, length us, event | category | flops | bytes accessed | tf_op | source)
XLA Modules:
  0.0 619.6 jit_solution(10360382922772073594)
XLA Ops:
  7.2 0.0 copy-start
  7.2 0.0 copy-start.7
  7.2 0.0 all-gather.3.cloned.1.call-start
  7.3 0.9 dynamic_slice.6
  8.2 0.0 copy-start.8
  8.2 1.0 broadcast_compare_fusion
  9.2 0.0 copy-start.14
  9.2 3.3 fusion.8
  12.5 0.0 copy-start.2
  12.5 3.2 copy-done.2
  15.7 0.0 copy-done.7
  15.7 4.6 fusion.4
  20.3 0.2 fusion.28
  20.5 0.0 copy-done
  20.5 0.0 copy-done.14
  20.5 11.6 %fusion = (f32[256,8]{0,1:T(8,128)S(1)}, f32[256,8,2048]{2,0,1:T(8,128)}) fusion(pred[256,2048]{1,0:T(8,128)(4,1)S(1)} %broadcast_compare_fusion, bf16[256,8,576]{0,2,1:T(8,128)(2,1)S(1)} %copy-done, bf16[2048,576]{0,1:T(8,128)(2,1)S(1)} %copy-done.14), kind=kOutput, calls=%fused_computation.3 | convolution fusion | flops 4844419072 | bytes 22028288 | tf_op jit(solution)/shard_map/dot_general | solution.py:17
  32.1 39.7 %all-reduce.1 = (f32[256,8]{0,1:T(8,128)S(1)}, f32[16]{0:T(128)S(1)}) all-reduce(f32[256,8]{0,1:T(8,128)S(1)} %get-tuple-element.7, f32[16]{0:T(128)S(1)} %fusion.28), channel_id=1, replica_groups=mesh['heads'=16,'keys'=16] {'keys'}, use_global_device_ids=true, to_apply=%region_5.6 | all-reduce | flops 2064 | bytes 16512 | tf_op jit(solution)/shard_map/pmax | solution.py:46
  71.8 0.0 copy-start.10
  71.9 0.0 copy-done.8
  71.9 0.2 fusion.29
  72.1 0.3 copy-done.10
  72.4 8.4 %fusion.1 = f32[256,8]{0,1:T(8,128)S(1)} fusion(f32[256,8,2048]{2,0,1:T(8,128)} %get-tuple-element.8, f32[256,8]{0,1:T(8,128)S(1)} %get-tuple-element.5, pred[256,2048]{1,0:T(8,128)(4,1)S(1)} %broadcast_compare_fusion), kind=kLoop, calls=%fused_computation.4 | loop fusion | flops 20969472 | bytes 17317888 | tf_op jit(solution)/shard_map/reduce_sum | solution.py:47
  80.7 31.5 %all-reduce = (f32[256,8]{0,1:T(8,128)S(1)}, f32[16]{0:T(128)}) all-reduce(f32[256,8]{0,1:T(8,128)S(1)} %fusion.1, f32[16]{0:T(128)S(1)} %fusion.29), channel_id=1, replica_groups=mesh['heads'=16,'keys'=16] {'keys'}, use_global_device_ids=true, to_apply=%region_7.8 | all-reduce | flops 2064 | bytes 16512 | tf_op jit(solution)/shard_map/psum | solution.py:53
  112.3 10.1 %divide_reduce_fusion = f32[256,2048]{1,0:T(8,128)} fusion(f32[256,8,2048]{2,0,1:T(8,128)} %get-tuple-element.8, f32[256,8]{0,1:T(8,128)S(1)} %get-tuple-element.3, f32[256,8]{0,1:T(8,128)S(1)} %get-tuple-element.5, pred[256,2048]{1,0:T(8,128)(4,1)S(1)} %broadcast_compare_fusion), kind=kLoop, calls=%fused_computation.2 | loop fusion | flops 24641536 | bytes 19415040 | tf_op jit(solution)/shard_map/reduce_sum | solution.py:58
  122.4 0.0 all-gather.3.cloned.1.call-update
  122.4 0.0 all-reduce.5.cloned.1.call-start
  122.5 185.6 %all-gather.3.cloned.1.call-done = f32[4096,2048]{1,0:T(8,128)} async-done(((f32[256,2048]{1,0:T(8,128)}), f32[4096,2048]{1,0:T(8,128)}) %all-gather.3.cloned.1.call-update) | async-done | bytes 33554448 | tf_op jit(solution)/shard_map/all_gather | solution.py:12
  308.1 0.0 copy-start.9
  308.1 0.0 copy-start.11
  308.1 0.0 copy-start.12
  308.1 0.0 copy-start.13
  308.1 0.0 copy-start.3
  308.1 0.0 copy-start.5
  308.1 11.9 %reduce_sum.39 = f32[256,2048]{1,0:T(8,128)S(1)} reduce(f32[16,256,2048]{2,1,0:T(8,128)} %bitcast.35, f32[]{:T(128)} %constant.11.clone.1), dimensions={0}, to_apply=%region_9.10 | reduce | flops 7864320 | bytes 35651588 | tf_op jit(solution)/shard_map/reduce_sum | solution.py:13
  320.0 0.0 copy-done.9
  320.0 0.0 copy-done.11
  320.1 0.0 copy-done.12
  320.1 0.0 copy-done.13
  320.1 0.1 subtract_multiply_fusion
  320.2 0.0 copy-done.3
  320.2 0.0 copy-done.5
  320.2 0.0 copy-start.4
  320.2 0.0 copy-start.6
  320.2 2.1 fusion.7
  322.3 0.0 all-reduce.5.cloned.1.call-update
  322.4 0.0 all-reduce.7.cloned.1.call-start
  322.4 0.0 copy-done.4
  322.4 0.0 copy-done.6
  322.4 0.0 copy-start.1
  322.5 2.6 fusion.19
  325.1 0.0 all-reduce.7.cloned.1.call-update
  325.1 9.0 %fusion.2 = f32[16,1,64]{2,1,0:T(1,128)S(1)} fusion(f32[16,64,2048]{2,1,0:T(8,128)} %copy-done.2, f32[16,2048,1]{1,0,2:T(8,128)S(1)} %bitcast.36), kind=kOutput, calls=%fused_computation.8 | convolution fusion | flops 27262976 | bytes 8523776 | tf_op jit(solution)/shard_map/qk,qjk->qj/dot_general | solution.py:67
  334.1 36.7 %psum.39 = f32[16,64]{1,0:T(8,128)} all-reduce(f32[16,64]{1,0:T(8,128)S(1)} %bitcast.37), channel_id=1, replica_groups=mesh['heads'=16,'keys'=16] {'keys'}, use_global_device_ids=true, to_apply=%region_12.13 | all-reduce | flops 1024 | bytes 8192 | tf_op jit(solution)/shard_map/psum | solution.py:81
  370.7 100.6 %all-reduce.5.cloned.1.call-done = f32[16,64,128]{2,1,0:T(8,128)} async-done(((f32[16,64,128]{2,1,0:T(8,128)}), f32[16,64,128]{2,1,0:T(8,128)}) %all-reduce.5.cloned.1.call-update) | async-done | bytes 524304 | tf_op jit(solution)/shard_map/psum | solution.py:81
  471.4 137.5 %all-reduce.7.cloned.1.call-done = f32[2048,128]{1,0:T(8,128)} async-done(((f32[2048,128]{1,0:T(8,128)}), f32[2048,128]{1,0:T(8,128)}) %all-reduce.7.cloned.1.call-update) | async-done | bytes 1048592 | tf_op jit(solution)/shard_map/psum | solution.py:82
  608.9 1.9 copy.27
  610.8 2.3 copy.28
  613.0 0.0 copy-done.1
  (1 shorter events, 0.0 us)
Async XLA Ops:
  7.2 13.4 %copy-start = (bf16[256,8,576]{0,2,1:T(8,128)(2,1)S(1)}, bf16[256,8,576]{0,2,1:T(8,128)(2,1)}, u32[]{:S(2)}) copy-start(bf16[256,8,576]{0,2,1:T(8,128)(2,1)} %param.7) | copy-start | bytes 7077892
  7.2 8.5 %copy-start.7 = (f32[16,64]{1,0:T(8,128)S(1)}, f32[16,64]{1,0:T(8,128)}, u32[]{:S(2)}) copy-start(f32[16,64]{1,0:T(8,128)} %param.11) | copy-start | bytes 12292
  7.2 300.9 %all-gather.3.cloned.1.call-start = ((), (), s32[]{:S(2)}) async-start(), calls=%async_computation.2 | async-start | bytes 35651584 | tf_op jit(solution)/shard_map/all_gather | solution.py:12
  8.2 63.7 %copy-start.8 = (s32[16]{0:T(128)}, s32[16]{0:T(128)S(1)}, u32[]{:S(2)}) copy-start(s32[16]{0:T(128)S(1)} %dynamic_slice.6) | copy-start | bytes 196
  9.2 11.3 %copy-start.14 = (bf16[2048,576]{0,1:T(8,128)(2,1)S(1)}, bf16[2048,576]{0,1:T(8,128)(2,1)}, u32[]{:S(2)}) copy-start(bf16[2048,576]{0,1:T(8,128)(2,1)} %param.8) | copy-start | bytes 7077892
  12.5 3.2 copy-start.2
  71.8 0.5 copy-start.10
  122.4 348.9 %all-reduce.5.cloned.1.call-start = ((), (), s32[]{:S(2)}) async-start(), calls=%async_computation | async-start | bytes 1048576 | tf_op jit(solution)/shard_map/psum | solution.py:81
  308.1 11.9 %copy-start.9 = (s32[16]{0:T(128)S(1)}, s32[16]{0:T(128)}, u32[]{:S(2)}) copy-start(s32[16]{0:T(128)} %copy-done.8) | copy-start | bytes 196
  308.1 11.9 %copy-start.11 = (f32[16]{0:T(128)S(1)}, f32[16]{0:T(128)}, u32[]{:S(2)}) copy-start(f32[16]{0:T(128)} %copy-done.10) | copy-start | bytes 196
  308.1 11.9 %copy-start.12 = (f32[16]{0:T(128)S(1)}, f32[16]{0:T(128)}, u32[]{:S(2)}) copy-start(f32[16]{0:T(128)} %param.13) | copy-start | bytes 196
  308.1 12.0 %copy-start.13 = (f32[16]{0:T(128)S(1)}, f32[16]{0:T(128)}, u32[]{:S(2)}) copy-start(f32[16]{0:T(128)} %get-tuple-element.4) | copy-start | bytes 196
  308.1 12.1 %copy-start.3 = (bf16[2048,128]{1,0:T(8,128)(2,1)S(1)}, bf16[2048,128]{1,0:T(8,128)(2,1)}, u32[]{:S(2)}) copy-start(bf16[2048,128]{1,0:T(8,128)(2,1)} %param.10) | copy-start | bytes 1572868
  308.1 12.1 %copy-start.5 = (u16[64,2048]{1,0:T(8,128)(2,1)S(1)}, u16[64,2048]{1,0:T(8,128)(2,1)}, u32[]{:S(2)}) copy-start(u16[64,2048]{1,0:T(8,128)(2,1)} %get-tuple-element.9) | copy-start | bytes 786436
  320.2 2.2 copy-start.4
  320.2 2.2 copy-start.6
  322.4 286.5 %all-reduce.7.cloned.1.call-start = ((), (), s32[]{:S(2)}) async-start(), calls=%async_computation.1 | async-start | bytes 2097152 | tf_op jit(solution)/shard_map/psum | solution.py:82
  322.4 290.6 %copy-start.1 = (bf16[256,8,576]{0,2,1:T(8,128)(2,1)S(1)}, bf16[256,8,576]{0,2,1:T(8,128)(2,1)}, u32[]{:S(2)}) copy-start(bf16[256,8,576]{0,2,1:T(8,128)(2,1)} %param.7) | copy-start | bytes 7077892
Sparse Core Ops, SparseCore 0:
  122.6 185.4 all-gather.2
  322.5 148.8 all-reduce.4
  474.6 134.2 all-reduce.6
